TPU v7x, 32 devices: a whole 2x2x4 slice. The times are simulated.
32 devices in a mesh: shard: 4 (over z), ctx: 2 (over core), tp: 4 (over y, x).
Axes of the slice: x: 2, y: 2, z: 4, core: 2. Of those that a mesh axis runs over, the one named last changes fastest.
Arguments:
- tokens: bfloat16 [8, 2048, 768], P('shard', 'ctx'), may hold values from -6 to 6
- segment_ids: int32 [8, 2048], P('shard', 'ctx'), may hold values from 0 to 34, as said below
- offsets: int32 [8, 2048], P('shard', 'ctx'), may hold values from 0 to 799, as said below
- qkv_weight: bfloat16 [768, 3, 768], P(('shard', 'ctx'), None, 'tp'), may hold values from -0.3125 to 0.3125
- out_weight: bfloat16 [768, 768], P(('shard', 'ctx'), 'tp'), may hold values from -0.875 to 0.875
- ffn_weight: bfloat16 [768, 2, 3072], P(('shard', 'ctx'), None, 'tp'), may hold values from -0.21875 to 0.21875
- qkv_bias: float32 [3, 768], P(None, 'tp'), may hold values from -3 to 3
- ffn_bias: float32 [3072], P('tp'), may hold values from -3 to 3
- norm_gain: float32 [2, 768], replicated, may hold values from 0.5 to 1.5
- shift_params: float32 [4, 768], replicated, may hold values from -3 to 3
- out_grad: bfloat16 [8, 2048, 768], P('shard', 'ctx'), may hold values from -6 to 6
Outputs:
- outputs: bfloat16 [8, 2048, 768], P('shard', 'ctx')
- grad_tokens: bfloat16 [8, 2048, 768], P('shard', 'ctx')
- grad_qkv_weight: float32 [768, 3, 768], P(('shard', 'ctx'), None, 'tp')
- grad_out_weight: float32 [768, 768], P(('shard', 'ctx'), 'tp')
- grad_ffn_weight: float32 [768, 2, 3072], P(('shard', 'ctx'), None, 'tp')
- grad_qkv_bias: float32 [3, 768], P(None, 'tp')
- grad_ffn_bias: float32 [3072], P('tp')
- grad_norm_gain: float32 [2, 768], replicated
- grad_shift_params: float32 [4, 768], replicated
Inputs may be any that keep to these rules, and one draw needn't show every extreme that they name: `segment_ids`: segment numbers start at 0 in each sequence and rise by one where a new document begins. offsets are 0 at a document's first token and rise by one along it; a document has at most 800 tokens, and every document but a sequence's last has at least 60.
All inputs are finite; a program needn't handle non-finite values.
Results may differ from a plain program's by a relative error of at most 0.017.
The roundings to bfloat16 on the way count: a program that leaves them out, or rounds other values in their place, can miss the bound.
Values may be sent and summed in bfloat16 or wider, within the bound.
No kernel may reach another device: no remote copies, remote signals or barrier semaphores. Data moves between devices by JAX's collectives and lax.ppermute only.
A program may use at most 192 MiB of HBM per device.

v0:
```python
from functools import partial
import jax
import jax.numpy as jnp
from jax import lax
from jax.sharding import PartitionSpec as P

HEAD = 64
EPSILON = 1e-12


def rotate_pairs(values, offsets, direction):
    half_size = values.shape[-1] // 2
    frequency = 10000.0 ** (-2.0 * jnp.arange(half_size, dtype=jnp.float32) / values.shape[-1])
    angles = offsets.astype(jnp.float32)[:, None] * frequency[None, :]
    cosine = jnp.cos(angles)[:, None, :]
    sine_part = direction * jnp.sin(angles)[:, None, :]
    paired = values.reshape(values.shape[:-1] + (half_size, 2))
    even_part = paired[..., 0]
    odd_part = paired[..., 1]
    turned = jnp.stack(
        [even_part * cosine - odd_part * sine_part, even_part * sine_part + odd_part * cosine],
        axis=-1,
    )
    return turned.reshape(values.shape)


def norm_parts(rows_in):
    centre = rows_in - jnp.mean(rows_in, axis=-1, keepdims=True)
    inverse_root = lax.rsqrt(jnp.mean(centre * centre, axis=-1, keepdims=True) + EPSILON)
    return (centre * inverse_root, inverse_root)


def norm_back(grad_in, scaled, inverse_root, gain_row):
    grad_scaled = grad_in * gain_row
    term_mean = jnp.mean(grad_scaled, axis=-1, keepdims=True)
    term_along = jnp.mean(grad_scaled * scaled, axis=-1, keepdims=True)
    return inverse_root * (grad_scaled - term_mean - scaled * term_along)


def attention_weights(qkv_weight, out_weight):
    return (
        lax.all_gather(qkv_weight, ("shard", "ctx"), axis=0, tiled=True),
        lax.all_gather(out_weight, ("shard", "ctx"), axis=0, tiled=True),
    )


def feed_weights(ffn_weight):
    return lax.all_gather(ffn_weight, ("shard", "ctx"), axis=0, tiled=True)


def masked_scores(queries, keys_all, same_doc, score_scale):
    scores = (
        jnp.einsum("shd,thd->hst", queries, keys_all, preferred_element_type=jnp.float32)
        * score_scale
    )
    return jnp.where(same_doc, scores, -1e30)


def contract_last(left, right):
    return lax.dot_general(
        left, right, (((1,), (1,)), ((), ())), preferred_element_type=jnp.float32
    )


def contract_first(left, right):
    return lax.dot_general(
        left, right, (((0,), (0,)), ((), ())), preferred_element_type=jnp.float32
    )


def body(
    tokens,
    segment_ids,
    offsets,
    qkv_weight,
    out_weight,
    ffn_weight,
    qkv_bias,
    ffn_bias,
    norm_gain,
    shift_params,
    out_grad,
):
    model_width = tokens.shape[2]
    part_width = qkv_weight.shape[2]
    hidden_width = ffn_weight.shape[2]
    local_heads = part_width // HEAD
    score_scale = HEAD ** (-0.5)
    tp_count = lax.axis_size("tp")
    tp_rank = lax.axis_index("tp")

    def micro_step(totals, micro_batch):
        tokens_mb, segment_mb, offsets_mb, grad_mb = micro_batch
        half_len = tokens_mb.shape[0]
        share_len = half_len // tp_count
        share_start = tp_rank * share_len

        def share_rows(rows):
            return lax.dynamic_slice_in_dim(rows, share_start, share_len, 0)

        qkv_full, out_full = attention_weights(qkv_weight, out_weight)
        ffn_full = feed_weights(ffn_weight)
        projected = (
            jnp.einsum("sd,dke->kse", tokens_mb, qkv_full, preferred_element_type=jnp.float32)
            + qkv_bias[:, None, :]
        )
        per_head = projected.reshape(3, half_len, local_heads, HEAD)
        queries = rotate_pairs(per_head[0], offsets_mb, 1.0).astype(jnp.bfloat16)
        keys_own = rotate_pairs(per_head[1], offsets_mb, 1.0).astype(jnp.bfloat16)
        values_own = per_head[2].astype(jnp.bfloat16)
        pair_own = jnp.stack([keys_own, values_own]).reshape(2, half_len, part_width)
        segment_own = segment_mb.astype(jnp.bfloat16)
        pair_all, segment_all = (
            lax.all_gather(pair_own, "ctx", axis=1, tiled=True),
            lax.all_gather(segment_own, "ctx", axis=0, tiled=True),
        )
        seq_len = pair_all.shape[1]
        keys_all = pair_all[0].reshape(seq_len, local_heads, HEAD)
        values_all = pair_all[1].reshape(seq_len, local_heads, HEAD)
        same_doc = (segment_own[:, None] == segment_all[None, :])[None]
        scores = masked_scores(queries, keys_all, same_doc, score_scale)
        row_top = jnp.max(scores, axis=-1, keepdims=True)
        exponent = jnp.exp(scores - row_top)
        row_total = jnp.sum(exponent, axis=-1, keepdims=True)
        probs_b = (exponent / row_total).astype(jnp.bfloat16)
        log_total = row_top + jnp.log(row_total)
        context = jnp.einsum(
            "hst,thd->shd", probs_b, values_all, preferred_element_type=jnp.float32
        )
        context = context.reshape(half_len, part_width).astype(jnp.bfloat16)
        attended = lax.psum(contract_last(context, out_full), "tp")
        first_scaled, first_root = norm_parts(
            tokens_mb.astype(jnp.float32) + attended + shift_params[2]
        )
        normed = first_scaled * norm_gain[0] + shift_params[0]
        normed_b = normed.astype(jnp.bfloat16)
        hidden_in = (
            jnp.dot(normed_b, ffn_full[:, 0, :], preferred_element_type=jnp.float32) + ffn_bias
        )
        activated, gelu_pull = jax.vjp(partial(jax.nn.gelu, approximate=False), hidden_in)
        activated_b = activated.astype(jnp.bfloat16)
        returned = lax.psum(contract_last(activated_b, ffn_full[:, 1, :]), "tp")
        second_scaled, second_root = norm_parts(normed + returned + shift_params[3])
        layer_out = (second_scaled * norm_gain[1] + shift_params[1]).astype(jnp.bfloat16)
        qkv_back, out_back = attention_weights(qkv_weight, out_weight)
        ffn_back = feed_weights(ffn_weight)
        grad_top = grad_mb.astype(jnp.float32)
        grad_gain_two = jnp.sum(share_rows(grad_top) * share_rows(second_scaled), axis=0)
        grad_second = norm_back(grad_top, second_scaled, second_root, norm_gain[1])
        grad_second_b = grad_second.astype(jnp.bfloat16)
        grad_down = contract_first(grad_second_b, activated_b)
        grad_act = jnp.dot(grad_second_b, ffn_back[:, 1, :], preferred_element_type=jnp.float32)
        grad_hidden = gelu_pull(grad_act)[0].astype(jnp.bfloat16)
        grad_up = contract_first(normed_b, grad_hidden)
        grad_ffn_bias = jnp.sum(grad_hidden.astype(jnp.float32), axis=0)
        ffn_part = contract_last(grad_hidden, ffn_back[:, 0, :])
        grad_normed = grad_second + lax.psum(ffn_part, "tp")
        grad_first = norm_back(grad_normed, first_scaled, first_root, norm_gain[0])
        grad_first_b = grad_first.astype(jnp.bfloat16)
        normed_part = share_rows(grad_normed)
        first_part = share_rows(grad_first)
        grad_gain_one = jnp.sum(normed_part * share_rows(first_scaled), axis=0)
        grad_out_proj = contract_first(grad_first_b, context)
        grad_context = jnp.dot(grad_first_b, out_back, preferred_element_type=jnp.float32).astype(
            jnp.bfloat16
        )
        grad_context = grad_context.reshape(half_len, local_heads, HEAD)
        scores_again = masked_scores(queries, keys_all, same_doc, score_scale)
        probs = jnp.exp(scores_again - log_total)
        probs_again = probs.astype(jnp.bfloat16)
        grad_probs = jnp.einsum(
            "shd,thd->hst", grad_context, values_all, preferred_element_type=jnp.float32
        )
        row_dot = jnp.sum(probs * grad_probs, axis=-1, keepdims=True)
        grad_scores = (probs * (grad_probs - row_dot)).astype(jnp.bfloat16)
        grad_queries = (
            jnp.einsum("hst,thd->shd", grad_scores, keys_all, preferred_element_type=jnp.float32)
            * score_scale
        )
        grad_keys = (
            jnp.einsum("hst,shd->thd", grad_scores, queries, preferred_element_type=jnp.float32)
            * score_scale
        )
        grad_values = jnp.einsum(
            "hst,shd->thd", probs_again, grad_context, preferred_element_type=jnp.float32
        )
        grad_pair = lax.psum_scatter(
            jnp.stack([grad_keys, grad_values]).reshape(2, seq_len, part_width),
            "ctx",
            scatter_dimension=1,
            tiled=True,
        )
        grad_pair = grad_pair.reshape(2, half_len, local_heads, HEAD)
        grad_proj = jnp.stack(
            [
                rotate_pairs(grad_queries, offsets_mb, -1.0),
                rotate_pairs(grad_pair[0], offsets_mb, -1.0),
                grad_pair[1],
            ]
        )
        grad_proj = grad_proj.reshape(3, half_len, part_width).astype(jnp.bfloat16)
        grad_qkv_bias = jnp.sum(grad_proj.astype(jnp.float32), axis=1)
        grad_qkv = jnp.einsum(
            "sd,kse->dke", tokens_mb, grad_proj, preferred_element_type=jnp.float32
        )
        grad_branch = jnp.einsum(
            "kse,dke->sd", grad_proj, qkv_back, preferred_element_type=jnp.float32
        )
        grad_inputs = (grad_first + lax.psum(grad_branch, "tp")).astype(jnp.bfloat16)
        grad_shift = jnp.stack(
            [
                jnp.sum(normed_part, axis=0),
                jnp.sum(share_rows(grad_top), axis=0),
                jnp.sum(first_part, axis=0),
                jnp.sum(share_rows(grad_second), axis=0),
            ]
        )
        grad_gain = jnp.stack([grad_gain_one, grad_gain_two])
        grad_ffn = jnp.stack([grad_up, grad_down], axis=1)
        updated = (
            totals[0] + grad_qkv,
            totals[1] + grad_out_proj,
            totals[2] + grad_ffn,
            totals[3] + grad_qkv_bias,
            totals[4] + grad_ffn_bias,
            totals[5] + grad_gain,
            totals[6] + grad_shift,
        )
        return (updated, (layer_out, grad_inputs))

    zero_grads = (
        jnp.zeros((model_width, 3, part_width), jnp.float32),
        jnp.zeros((model_width, part_width), jnp.float32),
        jnp.zeros((model_width, 2, hidden_width), jnp.float32),
        jnp.zeros((3, part_width), jnp.float32),
        jnp.zeros((hidden_width,), jnp.float32),
        jnp.zeros((2, model_width), jnp.float32),
        jnp.zeros((4, model_width), jnp.float32),
    )
    totals, (outputs, grad_tokens) = lax.scan(
        micro_step, zero_grads, (tokens, segment_ids, offsets, out_grad)
    )
    grad_qkv_weight, grad_out_weight, grad_ffn_weight = (
        lax.psum_scatter(totals[0], ("shard", "ctx"), scatter_dimension=0, tiled=True),
        lax.psum_scatter(totals[1], ("shard", "ctx"), scatter_dimension=0, tiled=True),
        lax.psum_scatter(totals[2], ("shard", "ctx"), scatter_dimension=0, tiled=True),
    )
    placed_qkv = lax.dynamic_update_slice(
        jnp.zeros((3, part_width * tp_count), jnp.float32),
        totals[3],
        (jnp.int32(0), tp_rank * part_width),
    )
    placed_ffn = lax.dynamic_update_slice(
        jnp.zeros((hidden_width * tp_count,), jnp.float32), totals[4], (tp_rank * hidden_width,)
    )
    summed_qkv, summed_ffn, grad_norm_gain, grad_shift_params = lax.psum(
        (placed_qkv, placed_ffn, totals[5], totals[6]), ("shard", "ctx", "tp")
    )
    grad_qkv_bias = lax.dynamic_slice_in_dim(summed_qkv, tp_rank * part_width, part_width, 1)
    grad_ffn_bias = lax.dynamic_slice_in_dim(summed_ffn, tp_rank * hidden_width, hidden_width, 0)
    return (
        outputs,
        grad_tokens,
        grad_qkv_weight,
        grad_out_weight,
        grad_ffn_weight,
        grad_qkv_bias,
        grad_ffn_bias,
        grad_norm_gain,
        grad_shift_params,
    )


def solution(mesh):
    return jax.shard_map(
        body,
        mesh=mesh,
        in_specs=(
            P("shard", "ctx", None),
            P("shard", "ctx"),
            P("shard", "ctx"),
            P(("shard", "ctx"), None, "tp"),
            P(("shard", "ctx"), "tp"),
            P(("shard", "ctx"), None, "tp"),
            P(None, "tp"),
            P("tp"),
            P(),
            P(),
            P("shard", "ctx", None),
        ),
        out_specs=(
            P("shard", "ctx", None),
            P("shard", "ctx", None),
            P(("shard", "ctx"), None, "tp"),
            P(("shard", "ctx"), "tp"),
            P(("shard", "ctx"), None, "tp"),
            P(None, "tp"),
            P("tp"),
            P(),
            P(),
        ),
        check_vma=False,
    )
```

profile of v0, /device:TPU:0, one launch (start us, length us, event | category | flops | bytes accessed | tf_op | source)
XLA Modules:
  0.0 1406.7 jit_solution(18068525269604240569)
XLA Ops:
  10.9 1200.5 %while.29 = (s32[]{:T(128)}, f32[768,3,192]{0,2,1:T(8,128)}, f32[768,192]{0,1:T(8,128)}, f32[768,2,768]{2,0,1:T(8,128)}, f32[3,192]{1,0:T(4,128)}, /*index=5*/f3...) while((s32[]{:T(128)}, f32[768,3,192]{0,2,1:T(8,128)}, ...), condition=%wide.region_25.26_spmd.clone, body=%wide.region_0.25_spmd.clone.sunk | while | flops 15947476992 | bytes 964769600 | solution.py:240
  10.9 23.1 %all_gather.42 = bf16[768,3,192]{2,1,0:T(4,128)(2,1)} all-gather(bf16[96,3,192]{2,1,0:T(4,128)(2,1)S(1)} %get-tuple-element.828), channel_id=1, replica_groups=mesh['shard'=4,'ctx'=2,'tp'=4] {'shard','ctx'}, dimensions={0}, use_global_device_ids=true | all-gather | bytes 995328 | tf_op jit(solution)/shard_map/while/body/eval_jaxpr/all_gather | solution.py:42
  34.0 3.4 copy.39
  48.1 4.2 subtract_convert_fusion.6
  58.0 2.8 pad_maximum_fusion.15
  63.8 16.3 %all_gather.41 = bf16[768,192]{1,0:T(8,128)(2,1)} all-gather(bf16[96,192]{1,0:T(8,128)(2,1)} %get-tuple-element.832), channel_id=1, replica_groups=mesh['shard'=4,'ctx'=2,'tp'=4] {'shard','ctx'}, dimensions={0}, use_global_device_ids=true | all-gather | bytes 331776 | tf_op jit(solution)/shard_map/while/body/eval_jaxpr/all_gather | solution.py:43
  84.7 11.0 fusion.150
  95.6 10.4 fusion.151
  106.1 10.6 fusion.152
  122.3 84.8 %all-reduce.10.cloned.1.call-done = f32[1024,768]{1,0:T(8,128)} async-done(((f32[1024,768]{1,0:T(8,128)}), f32[1024,768]{1,0:T(8,128)}) %all-reduce.10.cloned.1.call-update) | async-done | bytes 3145744 | tf_op jit(solution)/shard_map/while/body/eval_jaxpr/psum | solution.py:131
  207.0 2.5 fusion.154
  212.1 11.2 multiply_convert_fusion.4
  224.5 3.2 fusion.155
  228.0 87.1 %all-reduce.12.cloned.1.call-done = f32[1024,768]{1,0:T(8,128)} async-done(((f32[1024,768]{1,0:T(8,128)}), f32[1024,768]{1,0:T(8,128)}) %all-reduce.12.cloned.1.call-update) | async-done | bytes 3145744 | tf_op jit(solution)/shard_map/while/body/eval_jaxpr/psum | solution.py:142
  327.4 2.9 convert_reduce_fusion.4
  331.5 3.1 fusion.159
  335.9 86.1 %all-reduce.14.cloned.1.call-done = f32[1024,768]{1,0:T(8,128)} async-done(((f32[1024,768]{1,0:T(8,128)}), f32[1024,768]{1,0:T(8,128)}) %all-reduce.14.cloned.1.call-update) | async-done | bytes 3145744 | tf_op jit(solution)/shard_map/while/body/eval_jaxpr/psum | solution.py:157
  422.0 3.6 multiply_reduce_fusion.13
  430.4 11.4 fusion.160
  441.8 16.4 %multiply_reduce_fusion.14 = (f32[3,1024]{1,0:T(4,128)}, f32[3,1024,2048]{2,1,0:T(8,128)}) fusion(f32[3,1024,2048]{2,1,0:T(8,128)} %get-tuple-element.731, f32[3,1024]{1,0:T(4,128)S(1)} %log_add_fusion.2, bf16[1024,3,64]{0,2,1:T(8,128)(2,1)} %bitcast.223, bf16[2048,3,64]{0,2,1:T(8,128)(2,1)} %bitcast.227), kind=kOutput, calls=%fused_computation.1.clone.1 | convolution fusion | flops 824177664 | bytes 51535872 | tf_op jit(solution)/shard_map/while/body/eval_jaxpr/shd,thd->hst/dot_general | solution.py:171
  458.2 16.8 %multiply_convert_fusion.5 = bf16[3,1024,2048]{2,1,0:T(8,128)(2,1)S(1)} fusion(f32[3,1024,2048]{2,1,0:T(8,128)} %get-tuple-element.750, f32[3,1024,2048]{2,1,0:T(8,128)} %get-tuple-element.731, f32[3,1024]{1,0:T(4,128)} %get-tuple-element.751, f32[3,1024]{1,0:T(4,128)S(1)} %log_add_fusion.2), kind=kLoop, calls=%fused_computation.clone.1 | loop fusion | flops 25165824 | bytes 62939136 | tf_op jit(solution)/shard_map/while/body/eval_jaxpr/convert_element_type | solution.py:175
  485.2 10.5 fusion.161
  495.8 2.5 reshape.312
  502.9 3.8 subtract_convert_fusion.7
  506.7 2.7 pad_maximum_fusion.17
  516.0 3.1 convolution_bitcast_fusion.8
  521.3 4.0 convolution_bitcast_fusion.6
  536.2 70.3 %all-reduce.16.cloned.1.call-done = f32[1024,768]{1,0:T(8,128)} async-done(((f32[1024,768]{1,0:T(8,128)}), f32[1024,768]{1,0:T(8,128)}) %all-reduce.16.cloned.1.call-update) | async-done | bytes 3145744 | tf_op jit(solution)/shard_map/while/body/eval_jaxpr/psum | solution.py:209
  606.5 3.4 fusion.164
  610.1 21.4 %all_gather.42 = bf16[768,3,192]{2,1,0:T(4,128)(2,1)} all-gather(bf16[96,3,192]{2,1,0:T(4,128)(2,1)S(1)} %get-tuple-element.828), channel_id=1, replica_groups=mesh['shard'=4,'ctx'=2,'tp'=4] {'shard','ctx'}, dimensions={0}, use_global_device_ids=true | all-gather | bytes 995328 | tf_op jit(solution)/shard_map/while/body/eval_jaxpr/all_gather | solution.py:42
  631.5 3.4 copy.39
  645.6 4.2 subtract_convert_fusion.6
  655.5 2.8 pad_maximum_fusion.15
  661.3 16.0 %all_gather.41 = bf16[768,192]{1,0:T(8,128)(2,1)} all-gather(bf16[96,192]{1,0:T(8,128)(2,1)} %get-tuple-element.832), channel_id=1, replica_groups=mesh['shard'=4,'ctx'=2,'tp'=4] {'shard','ctx'}, dimensions={0}, use_global_device_ids=true | all-gather | bytes 331776 | tf_op jit(solution)/shard_map/while/body/eval_jaxpr/all_gather | solution.py:43
  681.8 11.0 fusion.150
  692.8 10.4 fusion.151
  703.3 10.6 fusion.152
  719.7 83.5 %all-reduce.10.cloned.1.call-done = f32[1024,768]{1,0:T(8,128)} async-done(((f32[1024,768]{1,0:T(8,128)}), f32[1024,768]{1,0:T(8,128)}) %all-reduce.10.cloned.1.call-update) | async-done | bytes 3145744 | tf_op jit(solution)/shard_map/while/body/eval_jaxpr/psum | solution.py:131
  803.2 2.5 fusion.154
  808.3 11.2 multiply_convert_fusion.4
  820.7 3.2 fusion.155
  824.1 87.2 %all-reduce.12.cloned.1.call-done = f32[1024,768]{1,0:T(8,128)} async-done(((f32[1024,768]{1,0:T(8,128)}), f32[1024,768]{1,0:T(8,128)}) %all-reduce.12.cloned.1.call-update) | async-done | bytes 3145744 | tf_op jit(solution)/shard_map/while/body/eval_jaxpr/psum | solution.py:142
  923.6 2.9 convert_reduce_fusion.4
  927.7 3.1 fusion.159
  931.9 86.4 %all-reduce.14.cloned.1.call-done = f32[1024,768]{1,0:T(8,128)} async-done(((f32[1024,768]{1,0:T(8,128)}), f32[1024,768]{1,0:T(8,128)}) %all-reduce.14.cloned.1.call-update) | async-done | bytes 3145744 | tf_op jit(solution)/shard_map/while/body/eval_jaxpr/psum | solution.py:157
  1018.2 3.6 multiply_reduce_fusion.13
  1026.6 11.4 fusion.160
  1038.0 16.4 %multiply_reduce_fusion.14 = (f32[3,1024]{1,0:T(4,128)}, f32[3,1024,2048]{2,1,0:T(8,128)}) fusion(f32[3,1024,2048]{2,1,0:T(8,128)} %get-tuple-element.731, f32[3,1024]{1,0:T(4,128)S(1)} %log_add_fusion.2, bf16[1024,3,64]{0,2,1:T(8,128)(2,1)} %bitcast.223, bf16[2048,3,64]{0,2,1:T(8,128)(2,1)} %bitcast.227), kind=kOutput, calls=%fused_computation.1.clone.1 | convolution fusion | flops 824177664 | bytes 51535872 | tf_op jit(solution)/shard_map/while/body/eval_jaxpr/shd,thd->hst/dot_general | solution.py:171
  1054.4 16.8 %multiply_convert_fusion.5 = bf16[3,1024,2048]{2,1,0:T(8,128)(2,1)S(1)} fusion(f32[3,1024,2048]{2,1,0:T(8,128)} %get-tuple-element.750, f32[3,1024,2048]{2,1,0:T(8,128)} %get-tuple-element.731, f32[3,1024]{1,0:T(4,128)} %get-tuple-element.751, f32[3,1024]{1,0:T(4,128)S(1)} %log_add_fusion.2), kind=kLoop, calls=%fused_computation.clone.1 | loop fusion | flops 25165824 | bytes 62939136 | tf_op jit(solution)/shard_map/while/body/eval_jaxpr/convert_element_type | solution.py:175
  1081.5 10.5 fusion.161
  1092.0 2.5 reshape.312
  1099.1 4.0 subtract_convert_fusion.7
  1103.2 2.7 pad_maximum_fusion.17
  1112.4 3.1 convolution_bitcast_fusion.8
  1117.8 4.0 convolution_bitcast_fusion.6
  1131.0 3.3 select_add_fusion.6
  1134.2 68.6 %all-reduce.16.cloned.1.call-done = f32[1024,768]{1,0:T(8,128)} async-done(((f32[1024,768]{1,0:T(8,128)}), f32[1024,768]{1,0:T(8,128)}) %all-reduce.16.cloned.1.call-update) | async-done | bytes 3145744 | tf_op jit(solution)/shard_map/while/body/eval_jaxpr/psum | solution.py:209
  1202.9 3.4 fusion.164
  1211.4 8.1 copy.37
  1221.9 3.0 copy.35
  1225.5 42.1 %all-reduce.1 = (f32[3,768]{1,0:T(4,128)S(1)}, f32[3072]{0:T(1024)S(1)}, f32[2,768]{1,0:T(2,128)}, f32[4,768]{1,0:T(4,128)}) all-reduce(f32[3,768]{1,0:T(4,128)S(1)} %dynamic_update_slice.19, f32[3072]{0:T(1024)S(1)} %dynamic_update_slice.20, ...), channel_id=1, replica_groups=mesh['shard'=4,'ctx'=2,'tp'=4] {'shard','ctx','tp'}, use_global_device_ids=true, to_apply=%region_29.30 | all-reduce | flops 9984 | bytes 79872 | tf_op jit(solution)/shard_map/psum | solution.py:256
  1270.2 56.7 %all-reduce.8.cloned.1.call-done = f32[768,2,768]{2,1,0:T(2,128)} async-done(((f32[768,2,768]{2,1,0:T(2,128)}), f32[768,2,768]{2,1,0:T(2,128)}) %all-reduce.8.cloned.1.call-update) | async-done | bytes 4718608
  1328.8 32.5 %reduce-scatter.6.cloned.1.call-done = f32[96,192]{1,0:T(8,128)} async-done(((f32[768,192]{1,0:T(8,128)}), f32[96,192]{1,0:T(8,128)}) %reduce-scatter.6.cloned.1.call-update) | async-done | bytes 73744 | tf_op jit(solution)/shard_map/reduce_scatter | solution.py:245
  1361.3 37.6 %reduce-scatter.4.cloned.1.call-done = f32[96,3,192]{2,0,1:T(8,128)} async-done(((f32[768,3,192]{2,0,1:T(8,128)}), f32[96,3,192]{2,0,1:T(8,128)}) %reduce-scatter.4.cloned.1.call-update) | async-done | bytes 221200 | tf_op jit(solution)/shard_map/reduce_scatter | solution.py:244
  (487 shorter events, 181.3 us)
Async XLA Ops:
  10.9 28.8 %copy-start.33 = (bf16[96,3,192]{2,1,0:T(4,128)(2,1)}, bf16[96,3,192]{2,1,0:T(4,128)(2,1)S(1)}, u32[]{:S(2)}) copy-start(bf16[96,3,192]{2,1,0:T(4,128)(2,1)S(1)} %get-tuple-element.828) | copy-start | bytes 331780 | tf_op jit(solution)/shard_map/while
  10.9 26.5 %copy-start.9 = (bf16[2,1024,768]{2,1,0:T(8,128)(2,1)S(1)}, bf16[2,1024,768]{2,1,0:T(8,128)(2,1)}, u32[]{:S(2)}) copy-start(bf16[2,1024,768]{2,1,0:T(8,128)(2,1)} %get-tuple-element.827) | copy-start | bytes 9437188 | tf_op jit(solution)/shard_map/while
  10.9 71.7 %all-gather.7.cloned.1.call-start = ((), (), s32[]{:S(2)}) async-start(), calls=%async_computation.6 | async-start | bytes 2359296 | tf_op jit(solution)/shard_map/while/body/eval_jaxpr/all_gather | solution.py:114
  52.4 9.5 copy-start.62
  57.9 149.1 %all-reduce.10.cloned.1.call-start = ((), (), s32[]{:S(2)}) async-start(), calls=%async_computation.7 | async-start | bytes 6291456 | tf_op jit(solution)/shard_map/while/body/eval_jaxpr/psum | solution.py:131
  84.2 11.4 copy-start.16
  84.2 21.9 %copy-start.20 = (bf16[1,2048,192]{1,2,0:T(8,128)(2,1)}, bf16[1,2048,192]{1,2,0:T(8,128)(2,1)S(1)}, u32[]{:S(2)}) copy-start(bf16[1,2048,192]{1,2,0:T(8,128)(2,1)S(1)} %get-tuple-element.725) | copy-start | bytes 2359300 | tf_op jit(solution)/shard_map/while
  95.6 10.5 copy-start.38
  106.1 10.7 copy-start.39
  106.1 11.4 copy-start.18
  119.9 92.2 %all-gather.9.cloned.1.call-start = ((), (), s32[]{:S(2)}) async-start(), calls=%async_computation.8 | async-start | bytes 2654208 | tf_op jit(solution)/shard_map/while/body/eval_jaxpr/all_gather | solution.py:48
  120.5 194.6 %all-reduce.12.cloned.1.call-start = ((), (), s32[]{:S(2)}) async-start(), calls=%async_computation.9 | async-start | bytes 6291456 | tf_op jit(solution)/shard_map/while/body/eval_jaxpr/psum | solution.py:142
  120.8 194.3 %copy-start.35 = (f32[768]{0:T(1024)}, f32[768]{0:T(1024)S(1)}, u32[]{:S(2)}) copy-start(f32[768]{0:T(1024)S(1)} %get-tuple-element.733) | copy-start | bytes 9220 | tf_op jit(solution)/shard_map/while
  122.3 192.8 %copy-start.45 = (f32[768]{0:T(1024)}, f32[768]{0:T(1024)S(1)}, u32[]{:S(2)}) copy-start(f32[768]{0:T(1024)S(1)} %get-tuple-element.737) | copy-start | bytes 9220 | tf_op jit(solution)/shard_map/while
  212.1 12.4 copy-start.65
  227.7 87.4 %copy-start.48 = (f32[768]{0:T(1024)S(1)}, f32[768]{0:T(1024)}, u32[]{:S(2)}) copy-start(f32[768]{0:T(1024)} %get-tuple-element.736) | copy-start | bytes 9220 | tf_op jit(solution)/shard_map/while
  227.7 194.3 %all-reduce.14.cloned.1.call-start = ((), (), s32[]{:S(2)}) async-start(), calls=%async_computation.10 | async-start | bytes 6291456 | tf_op jit(solution)/shard_map/while/body/eval_jaxpr/psum | solution.py:157
  322.9 4.5 copy-start.72
  324.0 6.4 copy-start.6
  334.7 163.7 %reduce-scatter.8.cloned.1.call-start = ((), (), s32[]{:S(2)}) async-start(), calls=%async_computation.11 | async-start | bytes 4718592 | tf_op jit(solution)/shard_map/while/body/eval_jaxpr/reduce_scatter | solution.py:187
  475.0 4.7 copy-start
  475.0 4.7 copy-start.8
  481.7 124.7 %all-reduce.16.cloned.1.call-start = ((), (), s32[]{:S(2)}) async-start(), calls=%async_computation.12 | async-start | bytes 6291456 | tf_op jit(solution)/shard_map/while/body/eval_jaxpr/psum | solution.py:209
  495.8 7.1 copy-start.27
  495.8 7.1 copy-start.32
  519.8 5.5 copy-start.54
  521.3 4.0 copy-start.37
  521.3 4.0 copy-start.46
  521.3 5.5 slice-start
  528.2 4.4 copy-start.14
  534.5 71.9 %copy-start.3 = (f32[1024,768]{1,0:T(8,128)S(1)}, f32[1024,768]{1,0:T(8,128)}, u32[]{:S(2)}) copy-start(f32[1024,768]{1,0:T(8,128)} %copy-done.1) | copy-start | bytes 9437188 | tf_op jit(solution)/shard_map/while
  610.0 27.2 %copy-start.33 = (bf16[96,3,192]{2,1,0:T(4,128)(2,1)}, bf16[96,3,192]{2,1,0:T(4,128)(2,1)S(1)}, u32[]{:S(2)}) copy-start(bf16[96,3,192]{2,1,0:T(4,128)(2,1)S(1)} %get-tuple-element.828) | copy-start | bytes 331780 | tf_op jit(solution)/shard_map/while
  610.0 24.9 %copy-start.9 = (bf16[2,1024,768]{2,1,0:T(8,128)(2,1)S(1)}, bf16[2,1024,768]{2,1,0:T(8,128)(2,1)}, u32[]{:S(2)}) copy-start(bf16[2,1024,768]{2,1,0:T(8,128)(2,1)} %get-tuple-element.827) | copy-start | bytes 9437188 | tf_op jit(solution)/shard_map/while
  610.0 69.7 %all-gather.7.cloned.1.call-start = ((), (), s32[]{:S(2)}) async-start(), calls=%async_computation.6 | async-start | bytes 2359296 | tf_op jit(solution)/shard_map/while/body/eval_jaxpr/all_gather | solution.py:114
  649.9 9.5 copy-start.62
  655.4 147.8 %all-reduce.10.cloned.1.call-start = ((), (), s32[]{:S(2)}) async-start(), calls=%async_computation.7 | async-start | bytes 6291456 | tf_op jit(solution)/shard_map/while/body/eval_jaxpr/psum | solution.py:131
  681.4 11.4 copy-start.16
  681.4 21.9 %copy-start.20 = (bf16[1,2048,192]{1,2,0:T(8,128)(2,1)}, bf16[1,2048,192]{1,2,0:T(8,128)(2,1)S(1)}, u32[]{:S(2)}) copy-start(bf16[1,2048,192]{1,2,0:T(8,128)(2,1)S(1)} %get-tuple-element.725) | copy-start | bytes 2359300 | tf_op jit(solution)/shard_map/while
  692.8 10.5 copy-start.38
  703.2 10.7 copy-start.39
  703.3 11.4 copy-start.18
  717.1 91.2 %all-gather.9.cloned.1.call-start = ((), (), s32[]{:S(2)}) async-start(), calls=%async_computation.8 | async-start | bytes 2654208 | tf_op jit(solution)/shard_map/while/body/eval_jaxpr/all_gather | solution.py:48
  717.7 193.6 %all-reduce.12.cloned.1.call-start = ((), (), s32[]{:S(2)}) async-start(), calls=%async_computation.9 | async-start | bytes 6291456 | tf_op jit(solution)/shard_map/while/body/eval_jaxpr/psum | solution.py:142
  718.2 193.0 %copy-start.35 = (f32[768]{0:T(1024)}, f32[768]{0:T(1024)S(1)}, u32[]{:S(2)}) copy-start(f32[768]{0:T(1024)S(1)} %get-tuple-element.733) | copy-start | bytes 9220 | tf_op jit(solution)/shard_map/while
  719.7 191.5 %copy-start.45 = (f32[768]{0:T(1024)}, f32[768]{0:T(1024)S(1)}, u32[]{:S(2)}) copy-start(f32[768]{0:T(1024)S(1)} %get-tuple-element.737) | copy-start | bytes 9220 | tf_op jit(solution)/shard_map/while
  808.3 12.4 copy-start.65
  823.9 87.4 %copy-start.48 = (f32[768]{0:T(1024)S(1)}, f32[768]{0:T(1024)}, u32[]{:S(2)}) copy-start(f32[768]{0:T(1024)} %get-tuple-element.736) | copy-start | bytes 9220 | tf_op jit(solution)/shard_map/while
  823.9 194.3 %all-reduce.14.cloned.1.call-start = ((), (), s32[]{:S(2)}) async-start(), calls=%async_computation.10 | async-start | bytes 6291456 | tf_op jit(solution)/shard_map/while/body/eval_jaxpr/psum | solution.py:157
  919.1 4.5 copy-start.72
  920.2 6.3 copy-start.6
  930.8 163.7 %reduce-scatter.8.cloned.1.call-start = ((), (), s32[]{:S(2)}) async-start(), calls=%async_computation.11 | async-start | bytes 4718592 | tf_op jit(solution)/shard_map/while/body/eval_jaxpr/reduce_scatter | solution.py:187
  1071.2 4.7 copy-start
  1071.2 4.7 copy-start.8
  1077.9 125.0 %all-reduce.16.cloned.1.call-start = ((), (), s32[]{:S(2)}) async-start(), calls=%async_computation.12 | async-start | bytes 6291456 | tf_op jit(solution)/shard_map/while/body/eval_jaxpr/psum | solution.py:209
  1092.0 7.1 copy-start.27
  1092.0 7.1 copy-start.32
  1116.3 5.5 copy-start.54
  1117.8 5.5 slice-start
  1124.7 4.4 copy-start.14
  1131.0 71.9 %copy-start.3 = (f32[1024,768]{1,0:T(8,128)S(1)}, f32[1024,768]{1,0:T(8,128)}, u32[]{:S(2)}) copy-start(f32[1024,768]{1,0:T(8,128)} %copy-done.1) | copy-start | bytes 9437188 | tf_op jit(solution)/shard_map/while
  1211.3 115.6 %all-reduce.8.cloned.1.call-start = ((), (), s32[]{:S(2)}) async-start(), calls=%async_computation.5 | async-start | bytes 9437184
  1219.5 141.8 %reduce-scatter.6.cloned.1.call-start = ((), (), s32[]{:S(2)}) async-start(), calls=%async_computation.4 | async-start | bytes 884736 | tf_op jit(solution)/shard_map/reduce_scatter | solution.py:245
  1221.8 177.1 %reduce-scatter.4.cloned.1.call-start = ((), (), s32[]{:S(2)}) async-start(), calls=%async_computation.3 | async-start | bytes 2654208 | tf_op jit(solution)/shard_map/reduce_scatter | solution.py:244
  1221.9 46.4 %copy-start.68 = (u32[32]{0:T(128)S(1)}, u32[32]{0:T(128)}, u32[]{:S(2)}) copy-start(u32[32]{0:T(128)} %constant.281) | copy-start | bytes 388
  (99 other events, 238.6 us)
Sparse Core Ops, SparseCore 0:
  58.0 9.4 all-gather.6
  120.0 86.9 all-reduce.9
  227.8 87.2 all-reduce.11
  334.8 87.1 all-reduce.13
  481.9 10.8 reduce-scatter.7
  519.3 87.1 all-reduce.15
  655.5 8.5 all-gather.6
  717.2 85.9 all-reduce.9
  824.0 87.2 all-reduce.11
  931.0 87.2 all-reduce.13
  1078.1 10.8 reduce-scatter.7
  1115.7 87.1 all-reduce.15
Sparse Core Ops, SparseCore 1:
  122.6 31.1 all-gather.8
  719.7 30.1 all-gather.8
  1219.6 107.2 all-reduce.7
  1329.8 31.5 reduce-scatter.5
  1364.3 34.5 reduce-scatter.3
where the time goes:
time: 1410 us
  waiting for transfers between devices  782 us (55%)
  matrix products  197 us (14%)
  other arithmetic  160 us (11%)
  blocking collectives  123 us (9%)
  local copies, waits for them, and re-layouts  119 us (8%)
  between operations  16.7 us (1%)
    psum x2, waiting for transfers between devices, micro_step(): returned = lax.psum(contract_last(activated_b, ffn_full[:, 1, :]), 'tp')  174 us
    psum x2, waiting for transfers between devices, micro_step(): grad_normed = grad_second + lax.psum(ffn_part, 'tp')  172 us
    psum x2, waiting for transfers between devices, micro_step(): attended = lax.psum(contract_last(context, out_full), 'tp')  168 us
    psum x2, waiting for transfers between devices, micro_step(): lax.psum(grad_branch, 'tp')  139 us
    unnamed x4, waiting for transfers between devices  56.7 us
    all_gather x2, blocking collectives, attention_weights(): lax.all_gather(qkv_weight, ('shard', 'ctx'), axis=0, tiled=True)  44.4 us
    while x280, local copies, waits for them, and re-layouts  43.6 us
    psum x1, blocking collectives, body(): lax.psum((placed_qkv, placed_ffn, totals[5], totals[6]), ('shard', 'ctx',...  42.1 us
  transfers between devices with their start and end apart: 17, of which 11 were waited for; matrix products, arithmetic and copies ran while one was open for 7% of the time, Pallas kernels for 0%

commit v1 on v0

--- a/solution.py
+++ b/solution.py
@@ -6,6 +6,22 @@
 
 HEAD = 64
 EPSILON = 1e-12
+
+
+def collect(x, axis, dim):
+    ways, here, lap = (lax.axis_size(axis), lax.axis_index(axis), x.shape[dim])
+    lengths = [n * ways if d == dim else n for d, n in enumerate(x.shape)]
+    full = lax.dynamic_update_slice_in_dim(jnp.zeros(lengths, x.dtype), x, here * lap, axis=dim)
+    going_up = going_down = x
+    for far in range(1, ways // 2 + 1):
+        going_up = lax.ppermute(going_up, axis, [(d, (d + 1) % ways) for d in range(ways)])
+        full = lax.dynamic_update_slice_in_dim(full, going_up, (here - far) % ways * lap, axis=dim)
+        if 2 * far < ways:
+            going_down = lax.ppermute(going_down, axis, [(d, (d - 1) % ways) for d in range(ways)])
+            full = lax.dynamic_update_slice_in_dim(
+                full, going_down, (here + far) % ways * lap, axis=dim
+            )
+    return full
 
 
 def rotate_pairs(values, offsets, direction):
@@ -40,7 +56,7 @@
 def attention_weights(qkv_weight, out_weight):
     return (
         lax.all_gather(qkv_weight, ("shard", "ctx"), axis=0, tiled=True),
-        lax.all_gather(out_weight, ("shard", "ctx"), axis=0, tiled=True),
+        collect(out_weight, ("shard", "ctx"), 0),
     )
 
 

time: 1410 us -> 1420 us (level)
  blocking collectives: 123 us -> 86.9 us
  local copies, waits for them, and re-layouts: 119 us -> 144 us
    all_gather x2 -> x0, blocking collectives: 32.2 us -> none  [attention_weights(): lax.all_gather(out_weight, ('shard', 'ctx'), axis=0, tiled=True)]
    dynamic_update_slice x0 -> x16, local copies, waits for them, and re-layouts: none -> 22.7 us  [the longest x8 11.3 us: collect(): lax.dynamic_update_slice_in_dim(full, going_up, (here - far) % ways * lap...]
    while x280 -> x272, local copies, waits for them, and re-layouts: 43.6 us -> 43.5 us
  transfers between devices with their start and end apart: 17 -> 24, of which waited for: 11 -> 15; matrix products, arithmetic and copies ran while one was open for 7% -> 9% of each run, Pallas kernels for 0% -> 0%
where the time goes in v1:
time: 1420 us
  waiting for transfers between devices  790 us (56%)
  matrix products  200 us (14%)
  other arithmetic  160 us (11%)
  local copies, waits for them, and re-layouts  144 us (10%)
  blocking collectives  86.9 us (6%)
  between operations  16.7 us (1%)
    psum x2, waiting for transfers between devices, micro_step(): returned = lax.psum(contract_last(activated_b, ffn_full[:, 1, :]), 'tp')  174 us
    psum x2, waiting for transfers between devices, micro_step(): grad_normed = grad_second + lax.psum(ffn_part, 'tp')  172 us
    psum x2, waiting for transfers between devices, micro_step(): attended = lax.psum(contract_last(context, out_full), 'tp')  168 us
    psum x2, waiting for transfers between devices, micro_step(): lax.psum(grad_branch, 'tp')  139 us
    unnamed x4, waiting for transfers between devices  56.7 us
    while x272, local copies, waits for them, and re-layouts  43.5 us
    psum x1, blocking collectives, body(): lax.psum((placed_qkv, placed_ffn, totals[5], totals[6]), ('shard', 'ctx',...  42.1 us
    all_gather x2, blocking collectives, attention_weights(): lax.all_gather(qkv_weight, ('shard', 'ctx'), axis=0, tiled=True)  40.2 us
  transfers between devices with their start and end apart: 24, of which 15 were waited for; matrix products, arithmetic and copies ran while one was open for 9% of the time, Pallas kernels for 0%

profile of v1, /device:TPU:0, one launch (start us, length us, event | category | flops | bytes accessed | tf_op | source)
XLA Modules:
  0.0 1419.4 jit_solution(9439125175515305674)
XLA Ops:
  8.5 4.1 collective-permute-start.1
  15.2 3.5 collective-permute-start.3
  21.2 3.3 collective-permute-start.5
  28.8 2.9 collective-permute-done.6
  31.7 1192.3 %while.29 = (s32[]{:T(128)}, f32[768,3,192]{0,2,1:T(8,128)}, f32[768,192]{0,1:T(8,128)}, f32[768,2,768]{2,0,1:T(8,128)}, f32[3,192]{1,0:T(4,128)}, /*index=5*/f3...) while((s32[]{:T(128)}, f32[768,3,192]{0,2,1:T(8,128)}, ...), condition=%wide.region_25.26_spmd.clone, body=%wide.region_0.25_spmd.clone.sunk | while | flops 15947476992 | bytes 963161344 | solution.py:256
  31.7 18.8 %all_gather.32 = bf16[768,3,192]{2,1,0:T(4,128)(2,1)} all-gather(bf16[96,3,192]{2,1,0:T(4,128)(2,1)S(1)} %get-tuple-element.1010), channel_id=1, replica_groups=mesh['shard'=4,'ctx'=2,'tp'=4] {'shard','ctx'}, dimensions={0}, use_global_device_ids=true | all-gather | bytes 995328 | tf_op jit(solution)/shard_map/while/body/eval_jaxpr/all_gather | solution.py:58
  50.6 3.4 copy.39
  64.7 4.2 subtract_convert_fusion.6
  74.5 2.8 pad_maximum_fusion.15
  97.6 11.0 fusion.155
  108.6 10.4 fusion.156
  119.1 10.6 fusion.157
  130.4 3.3 fusion.158
  136.1 84.7 %all-reduce.10.cloned.1.call-done = f32[1024,768]{1,0:T(8,128)} async-done(((f32[1024,768]{1,0:T(8,128)}), f32[1024,768]{1,0:T(8,128)}) %all-reduce.10.cloned.1.call-update) | async-done | bytes 3145744 | tf_op jit(solution)/shard_map/while/body/eval_jaxpr/psum | solution.py:147
  225.9 11.2 multiply_convert_fusion.4
  238.3 3.1 fusion.160
  241.7 87.1 %all-reduce.12.cloned.1.call-done = f32[1024,768]{1,0:T(8,128)} async-done(((f32[1024,768]{1,0:T(8,128)}), f32[1024,768]{1,0:T(8,128)}) %all-reduce.12.cloned.1.call-update) | async-done | bytes 3145744 | tf_op jit(solution)/shard_map/while/body/eval_jaxpr/psum | solution.py:158
  341.1 2.9 convert_reduce_fusion.4
  345.2 3.1 fusion.164
  349.5 86.1 %all-reduce.14.cloned.1.call-done = f32[1024,768]{1,0:T(8,128)} async-done(((f32[1024,768]{1,0:T(8,128)}), f32[1024,768]{1,0:T(8,128)}) %all-reduce.14.cloned.1.call-update) | async-done | bytes 3145744 | tf_op jit(solution)/shard_map/while/body/eval_jaxpr/psum | solution.py:173
  435.7 3.6 multiply_reduce_fusion.13
  445.0 11.4 fusion.165
  456.4 16.5 %multiply_reduce_fusion.14 = (f32[3,1024]{1,0:T(4,128)}, f32[3,1024,2048]{2,1,0:T(8,128)}) fusion(f32[3,1024,2048]{2,1,0:T(8,128)} %get-tuple-element.871, f32[3,1024]{1,0:T(4,128)S(1)} %log_add_fusion.2, bf16[1024,3,64]{0,2,1:T(8,128)(2,1)} %bitcast.223, bf16[2048,3,64]{0,2,1:T(8,128)(2,1)} %bitcast.227), kind=kOutput, calls=%fused_computation.1.clone.1 | convolution fusion | flops 824177664 | bytes 51535872 | tf_op jit(solution)/shard_map/while/body/eval_jaxpr/shd,thd->hst/dot_general | solution.py:187
  473.0 16.8 %multiply_convert_fusion.5 = bf16[3,1024,2048]{2,1,0:T(8,128)(2,1)S(1)} fusion(f32[3,1024,2048]{2,1,0:T(8,128)} %get-tuple-element.890, f32[3,1024,2048]{2,1,0:T(8,128)} %get-tuple-element.871, f32[3,1024]{1,0:T(4,128)} %get-tuple-element.891, f32[3,1024]{1,0:T(4,128)S(1)} %log_add_fusion.2), kind=kLoop, calls=%fused_computation.clone.1 | loop fusion | flops 25165824 | bytes 62939136 | tf_op jit(solution)/shard_map/while/body/eval_jaxpr/convert_element_type | solution.py:191
  500.1 10.5 fusion.166
  517.7 3.8 subtract_convert_fusion.7
  521.5 2.7 pad_maximum_fusion.17
  530.7 3.1 convolution_bitcast_fusion.8
  536.0 4.0 convolution_bitcast_fusion.6
  550.8 70.2 %all-reduce.16.cloned.1.call-done = f32[1024,768]{1,0:T(8,128)} async-done(((f32[1024,768]{1,0:T(8,128)}), f32[1024,768]{1,0:T(8,128)}) %all-reduce.16.cloned.1.call-update) | async-done | bytes 3145744 | tf_op jit(solution)/shard_map/while/body/eval_jaxpr/psum | solution.py:225
  621.1 3.4 fusion.169
  624.8 21.4 %all_gather.32 = bf16[768,3,192]{2,1,0:T(4,128)(2,1)} all-gather(bf16[96,3,192]{2,1,0:T(4,128)(2,1)S(1)} %get-tuple-element.1010), channel_id=1, replica_groups=mesh['shard'=4,'ctx'=2,'tp'=4] {'shard','ctx'}, dimensions={0}, use_global_device_ids=true | all-gather | bytes 995328 | tf_op jit(solution)/shard_map/while/body/eval_jaxpr/all_gather | solution.py:58
  646.1 3.4 copy.39
  660.3 4.2 subtract_convert_fusion.6
  670.0 2.8 pad_maximum_fusion.15
  692.8 11.0 fusion.155
  703.8 10.4 fusion.156
  714.3 10.6 fusion.157
  725.6 3.3 fusion.158
  731.6 83.4 %all-reduce.10.cloned.1.call-done = f32[1024,768]{1,0:T(8,128)} async-done(((f32[1024,768]{1,0:T(8,128)}), f32[1024,768]{1,0:T(8,128)}) %all-reduce.10.cloned.1.call-update) | async-done | bytes 3145744 | tf_op jit(solution)/shard_map/while/body/eval_jaxpr/psum | solution.py:147
  820.2 11.2 multiply_convert_fusion.4
  832.5 3.1 fusion.160
  835.9 87.2 %all-reduce.12.cloned.1.call-done = f32[1024,768]{1,0:T(8,128)} async-done(((f32[1024,768]{1,0:T(8,128)}), f32[1024,768]{1,0:T(8,128)}) %all-reduce.12.cloned.1.call-update) | async-done | bytes 3145744 | tf_op jit(solution)/shard_map/while/body/eval_jaxpr/psum | solution.py:158
  935.3 2.9 convert_reduce_fusion.4
  939.4 3.1 fusion.164
  943.6 86.3 %all-reduce.14.cloned.1.call-done = f32[1024,768]{1,0:T(8,128)} async-done(((f32[1024,768]{1,0:T(8,128)}), f32[1024,768]{1,0:T(8,128)}) %all-reduce.14.cloned.1.call-update) | async-done | bytes 3145744 | tf_op jit(solution)/shard_map/while/body/eval_jaxpr/psum | solution.py:173
  1029.9 3.6 multiply_reduce_fusion.13
  1039.2 11.4 fusion.165
  1050.6 16.5 %multiply_reduce_fusion.14 = (f32[3,1024]{1,0:T(4,128)}, f32[3,1024,2048]{2,1,0:T(8,128)}) fusion(f32[3,1024,2048]{2,1,0:T(8,128)} %get-tuple-element.871, f32[3,1024]{1,0:T(4,128)S(1)} %log_add_fusion.2, bf16[1024,3,64]{0,2,1:T(8,128)(2,1)} %bitcast.223, bf16[2048,3,64]{0,2,1:T(8,128)(2,1)} %bitcast.227), kind=kOutput, calls=%fused_computation.1.clone.1 | convolution fusion | flops 824177664 | bytes 51535872 | tf_op jit(solution)/shard_map/while/body/eval_jaxpr/shd,thd->hst/dot_general | solution.py:187
  1067.2 16.8 %multiply_convert_fusion.5 = bf16[3,1024,2048]{2,1,0:T(8,128)(2,1)S(1)} fusion(f32[3,1024,2048]{2,1,0:T(8,128)} %get-tuple-element.890, f32[3,1024,2048]{2,1,0:T(8,128)} %get-tuple-element.871, f32[3,1024]{1,0:T(4,128)} %get-tuple-element.891, f32[3,1024]{1,0:T(4,128)S(1)} %log_add_fusion.2), kind=kLoop, calls=%fused_computation.clone.1 | loop fusion | flops 25165824 | bytes 62939136 | tf_op jit(solution)/shard_map/while/body/eval_jaxpr/convert_element_type | solution.py:191
  1094.3 10.5 fusion.166
  1111.9 4.0 subtract_convert_fusion.7
  1115.9 2.7 pad_maximum_fusion.17
  1125.1 3.1 convolution_bitcast_fusion.8
  1130.4 4.0 convolution_bitcast_fusion.6
  1143.6 3.3 select_add_fusion.6
  1146.9 68.6 %all-reduce.16.cloned.1.call-done = f32[1024,768]{1,0:T(8,128)} async-done(((f32[1024,768]{1,0:T(8,128)}), f32[1024,768]{1,0:T(8,128)}) %all-reduce.16.cloned.1.call-update) | async-done | bytes 3145744 | tf_op jit(solution)/shard_map/while/body/eval_jaxpr/psum | solution.py:225
  1215.5 3.4 fusion.169
  1224.0 8.1 copy.37
  1234.6 3.0 copy.35
  1239.5 42.1 %all-reduce.1 = (f32[3,768]{1,0:T(4,128)S(1)}, f32[3072]{0:T(1024)S(1)}, f32[2,768]{1,0:T(2,128)}, f32[4,768]{1,0:T(4,128)}) all-reduce(f32[3,768]{1,0:T(4,128)S(1)} %dynamic_update_slice.75, f32[3072]{0:T(1024)S(1)} %dynamic_update_slice.76, ...), channel_id=1, replica_groups=mesh['shard'=4,'ctx'=2,'tp'=4] {'shard','ctx','tp'}, use_global_device_ids=true, to_apply=%region_29.30 | all-reduce | flops 9984 | bytes 79872 | tf_op jit(solution)/shard_map/psum | solution.py:272
  1282.9 56.6 %all-reduce.8.cloned.1.call-done = f32[768,2,768]{2,1,0:T(2,128)} async-done(((f32[768,2,768]{2,1,0:T(2,128)}), f32[768,2,768]{2,1,0:T(2,128)}) %all-reduce.8.cloned.1.call-update) | async-done | bytes 4718608
  1341.5 32.5 %reduce-scatter.6.cloned.1.call-done = f32[96,192]{1,0:T(8,128)} async-done(((f32[768,192]{1,0:T(8,128)}), f32[96,192]{1,0:T(8,128)}) %reduce-scatter.6.cloned.1.call-update) | async-done | bytes 73744 | tf_op jit(solution)/shard_map/reduce_scatter | solution.py:261
  1374.0 37.6 %reduce-scatter.4.cloned.1.call-done = f32[96,3,192]{2,0,1:T(8,128)} async-done(((f32[768,3,192]{2,0,1:T(8,128)}), f32[96,3,192]{2,0,1:T(8,128)}) %reduce-scatter.4.cloned.1.call-update) | async-done | bytes 221200 | tf_op jit(solution)/shard_map/reduce_scatter | solution.py:260
  (515 shorter events, 220.6 us)
Async XLA Ops:
  8.0 6.5 collective-permute-start
  8.5 6.7 collective-permute-start.1
  15.2 5.4 collective-permute-start.2
  15.2 5.4 copy-start.39
  15.2 5.4 collective-permute-start.3
  20.6 5.4 collective-permute-start.4
  21.2 7.6 collective-permute-start.5
  26.0 5.7 collective-permute-start.6
  31.7 24.6 %copy-start.31 = (bf16[96,3,192]{2,1,0:T(4,128)(2,1)}, bf16[96,3,192]{2,1,0:T(4,128)(2,1)S(1)}, u32[]{:S(2)}) copy-start(bf16[96,3,192]{2,1,0:T(4,128)(2,1)S(1)} %get-tuple-element.1010) | copy-start | bytes 331780 | tf_op jit(solution)/shard_map/while
  31.7 22.3 %copy-start.9 = (bf16[2,1024,768]{2,1,0:T(8,128)(2,1)S(1)}, bf16[2,1024,768]{2,1,0:T(8,128)(2,1)}, u32[]{:S(2)}) copy-start(bf16[2,1024,768]{2,1,0:T(8,128)(2,1)} %get-tuple-element.1009) | copy-start | bytes 9437188 | tf_op jit(solution)/shard_map/while
  31.7 63.9 %all-gather.7.cloned.1.call-start = ((), (), s32[]{:S(2)}) async-start(), calls=%async_computation.6 | async-start | bytes 2359296 | tf_op jit(solution)/shard_map/while/body/eval_jaxpr/all_gather | solution.py:130
  68.9 9.5 copy-start.63
  74.4 146.5 %all-reduce.10.cloned.1.call-start = ((), (), s32[]{:S(2)}) async-start(), calls=%async_computation.7 | async-start | bytes 6291456 | tf_op jit(solution)/shard_map/while/body/eval_jaxpr/psum | solution.py:147
  97.2 11.4 copy-start.16
  97.2 21.8 %copy-start.18 = (bf16[1,2048,192]{1,2,0:T(8,128)(2,1)}, bf16[1,2048,192]{1,2,0:T(8,128)(2,1)S(1)}, u32[]{:S(2)}) copy-start(bf16[1,2048,192]{1,2,0:T(8,128)(2,1)S(1)} %get-tuple-element.865) | copy-start | bytes 2359300 | tf_op jit(solution)/shard_map/while
  108.6 10.5 copy-start.36
  119.0 10.6 copy-start.37
  133.8 92.2 %all-gather.9.cloned.1.call-start = ((), (), s32[]{:S(2)}) async-start(), calls=%async_computation.8 | async-start | bytes 2654208 | tf_op jit(solution)/shard_map/while/body/eval_jaxpr/all_gather | solution.py:64
  134.3 194.5 %all-reduce.12.cloned.1.call-start = ((), (), s32[]{:S(2)}) async-start(), calls=%async_computation.9 | async-start | bytes 6291456 | tf_op jit(solution)/shard_map/while/body/eval_jaxpr/psum | solution.py:158
  134.6 194.2 %copy-start.33 = (f32[768]{0:T(1024)}, f32[768]{0:T(1024)S(1)}, u32[]{:S(2)}) copy-start(f32[768]{0:T(1024)S(1)} %get-tuple-element.873) | copy-start | bytes 9220 | tf_op jit(solution)/shard_map/while
  136.1 192.7 %copy-start.46 = (f32[768]{0:T(1024)}, f32[768]{0:T(1024)S(1)}, u32[]{:S(2)}) copy-start(f32[768]{0:T(1024)S(1)} %get-tuple-element.877) | copy-start | bytes 9220 | tf_op jit(solution)/shard_map/while
  225.9 12.3 copy-start.66
  241.4 87.4 %copy-start.49 = (f32[768]{0:T(1024)S(1)}, f32[768]{0:T(1024)}, u32[]{:S(2)}) copy-start(f32[768]{0:T(1024)} %get-tuple-element.876) | copy-start | bytes 9220 | tf_op jit(solution)/shard_map/while
  241.4 194.2 %all-reduce.14.cloned.1.call-start = ((), (), s32[]{:S(2)}) async-start(), calls=%async_computation.10 | async-start | bytes 6291456 | tf_op jit(solution)/shard_map/while/body/eval_jaxpr/psum | solution.py:173
  337.7 6.3 copy-start.6
  348.3 164.8 %reduce-scatter.8.cloned.1.call-start = ((), (), s32[]{:S(2)}) async-start(), calls=%async_computation.11 | async-start | bytes 4718592 | tf_op jit(solution)/shard_map/while/body/eval_jaxpr/reduce_scatter | solution.py:203
  489.8 4.7 copy-start
  489.8 4.7 copy-start.8
  496.5 124.6 %all-reduce.16.cloned.1.call-start = ((), (), s32[]{:S(2)}) async-start(), calls=%async_computation.12 | async-start | bytes 6291456 | tf_op jit(solution)/shard_map/while/body/eval_jaxpr/psum | solution.py:225
  510.6 7.1 copy-start.25
  510.6 7.1 copy-start.30
  534.5 5.5 copy-start.55
  536.0 5.5 slice-start
  549.2 71.9 %copy-start.3 = (f32[1024,768]{1,0:T(8,128)S(1)}, f32[1024,768]{1,0:T(8,128)}, u32[]{:S(2)}) copy-start(f32[1024,768]{1,0:T(8,128)} %copy-done.1) | copy-start | bytes 9437188 | tf_op jit(solution)/shard_map/while
  624.7 27.2 %copy-start.31 = (bf16[96,3,192]{2,1,0:T(4,128)(2,1)}, bf16[96,3,192]{2,1,0:T(4,128)(2,1)S(1)}, u32[]{:S(2)}) copy-start(bf16[96,3,192]{2,1,0:T(4,128)(2,1)S(1)} %get-tuple-element.1010) | copy-start | bytes 331780 | tf_op jit(solution)/shard_map/while
  624.7 24.9 %copy-start.9 = (bf16[2,1024,768]{2,1,0:T(8,128)(2,1)S(1)}, bf16[2,1024,768]{2,1,0:T(8,128)(2,1)}, u32[]{:S(2)}) copy-start(bf16[2,1024,768]{2,1,0:T(8,128)(2,1)} %get-tuple-element.1009) | copy-start | bytes 9437188 | tf_op jit(solution)/shard_map/while
  624.7 66.1 %all-gather.7.cloned.1.call-start = ((), (), s32[]{:S(2)}) async-start(), calls=%async_computation.6 | async-start | bytes 2359296 | tf_op jit(solution)/shard_map/while/body/eval_jaxpr/all_gather | solution.py:130
  664.4 9.5 copy-start.63
  670.0 145.1 %all-reduce.10.cloned.1.call-start = ((), (), s32[]{:S(2)}) async-start(), calls=%async_computation.7 | async-start | bytes 6291456 | tf_op jit(solution)/shard_map/while/body/eval_jaxpr/psum | solution.py:147
  692.4 11.4 copy-start.16
  692.4 21.8 %copy-start.18 = (bf16[1,2048,192]{1,2,0:T(8,128)(2,1)}, bf16[1,2048,192]{1,2,0:T(8,128)(2,1)S(1)}, u32[]{:S(2)}) copy-start(bf16[1,2048,192]{1,2,0:T(8,128)(2,1)S(1)} %get-tuple-element.865) | copy-start | bytes 2359300 | tf_op jit(solution)/shard_map/while
  703.8 10.5 copy-start.36
  714.2 10.6 copy-start.37
  729.0 91.1 %all-gather.9.cloned.1.call-start = ((), (), s32[]{:S(2)}) async-start(), calls=%async_computation.8 | async-start | bytes 2654208 | tf_op jit(solution)/shard_map/while/body/eval_jaxpr/all_gather | solution.py:64
  729.6 193.4 %all-reduce.12.cloned.1.call-start = ((), (), s32[]{:S(2)}) async-start(), calls=%async_computation.9 | async-start | bytes 6291456 | tf_op jit(solution)/shard_map/while/body/eval_jaxpr/psum | solution.py:158
  730.1 192.9 %copy-start.33 = (f32[768]{0:T(1024)}, f32[768]{0:T(1024)S(1)}, u32[]{:S(2)}) copy-start(f32[768]{0:T(1024)S(1)} %get-tuple-element.873) | copy-start | bytes 9220 | tf_op jit(solution)/shard_map/while
  731.6 191.4 %copy-start.46 = (f32[768]{0:T(1024)}, f32[768]{0:T(1024)S(1)}, u32[]{:S(2)}) copy-start(f32[768]{0:T(1024)S(1)} %get-tuple-element.877) | copy-start | bytes 9220 | tf_op jit(solution)/shard_map/while
  820.1 12.3 copy-start.66
  835.6 87.4 %copy-start.49 = (f32[768]{0:T(1024)S(1)}, f32[768]{0:T(1024)}, u32[]{:S(2)}) copy-start(f32[768]{0:T(1024)} %get-tuple-element.876) | copy-start | bytes 9220 | tf_op jit(solution)/shard_map/while
  835.7 194.2 %all-reduce.14.cloned.1.call-start = ((), (), s32[]{:S(2)}) async-start(), calls=%async_computation.10 | async-start | bytes 6291456 | tf_op jit(solution)/shard_map/while/body/eval_jaxpr/psum | solution.py:173
  931.9 6.3 copy-start.6
  942.5 164.8 %reduce-scatter.8.cloned.1.call-start = ((), (), s32[]{:S(2)}) async-start(), calls=%async_computation.11 | async-start | bytes 4718592 | tf_op jit(solution)/shard_map/while/body/eval_jaxpr/reduce_scatter | solution.py:203
  1084.0 4.7 copy-start
  1090.7 124.8 %all-reduce.16.cloned.1.call-start = ((), (), s32[]{:S(2)}) async-start(), calls=%async_computation.12 | async-start | bytes 6291456 | tf_op jit(solution)/shard_map/while/body/eval_jaxpr/psum | solution.py:225
  1104.8 7.1 copy-start.25
  1104.8 7.1 copy-start.30
  1128.9 5.5 copy-start.55
  1130.4 5.5 slice-start
  1143.6 71.9 %copy-start.3 = (f32[1024,768]{1,0:T(8,128)S(1)}, f32[1024,768]{1,0:T(8,128)}, u32[]{:S(2)}) copy-start(f32[1024,768]{1,0:T(8,128)} %copy-done.1) | copy-start | bytes 9437188 | tf_op jit(solution)/shard_map/while
  1224.0 115.6 %all-reduce.8.cloned.1.call-start = ((), (), s32[]{:S(2)}) async-start(), calls=%async_computation.5 | async-start | bytes 9437184
  1232.2 141.8 %reduce-scatter.6.cloned.1.call-start = ((), (), s32[]{:S(2)}) async-start(), calls=%async_computation.4 | async-start | bytes 884736 | tf_op jit(solution)/shard_map/reduce_scatter | solution.py:261
  1234.4 177.1 %reduce-scatter.4.cloned.1.call-start = ((), (), s32[]{:S(2)}) async-start(), calls=%async_computation.3 | async-start | bytes 2654208 | tf_op jit(solution)/shard_map/reduce_scatter | solution.py:260
  1234.5 4.9 copy-start.45
  1234.5 4.9 copy-start.52
  (105 other events, 264.0 us)
Sparse Core Ops, SparseCore 0:
  74.5 9.5 all-gather.6
  133.9 86.9 all-reduce.9
  241.6 87.2 all-reduce.11
  348.5 87.1 all-reduce.13
  496.6 10.8 reduce-scatter.7
  533.9 87.1 all-reduce.15
  670.1 8.5 all-gather.6
  729.1 85.9 all-reduce.9
  835.8 87.2 all-reduce.11
  942.7 87.1 all-reduce.13
  1090.8 10.8 reduce-scatter.7
  1128.4 87.1 all-reduce.15
Sparse Core Ops, SparseCore 1:
  136.4 31.1 all-gather.8
  731.7 30.1 all-gather.8
  1232.3 107.2 all-reduce.7
  1342.4 31.5 reduce-scatter.5
  1377.0 34.5 reduce-scatter.3
